TPU v7x, 32 devices: a whole 2x2x4 slice. The times are simulated.
32 devices in a mesh: groups: 2 (over x), cx: 16 (over z, y, core).
Axes of the slice: x: 2, y: 2, z: 4, core: 2. Of those that a mesh axis runs over, the one named last changes fastest.
Arguments:
- displacements: bfloat16 [512, 3, 5120], P(('groups', 'cx')), parts along dimension 0, may hold values from -6 to 6
- forces: bfloat16 [512, 3, 5120], P(('groups', 'cx')), parts along dimension 0, may hold values from -6 to 6
- phi: bfloat16 [160, 14, 192, 192], P(('groups', 'cx')), parts along dimension 0, may hold values from -0.125 to 0.125
- neighbours: int32 [80, 14], P('cx'), may hold values from 0 to 79, as said below
- cluster_atoms: int32 [80, 64], P('cx'), may hold values from 0 to 5119, as said below
- config_order: int32 [512], P('groups'), parts along dimension 0, may hold values from 0 to 255, each once
- weights: float32 [512], P('groups'), parts along dimension 0, may hold values from 0.02 to 0.3
Outputs:
- residual: bfloat16 [160, 192, 256], P(('groups', 'cx')), parts along dimension 0
- gradient: bfloat16 [160, 14, 192, 192], P(('groups', 'cx')), parts along dimension 0
There are 2 independent parts, one for each index of `groups`. A program takes and returns all parts, laid end to end along the dimension named above; an argument that names none is the same for every part. Nothing has to cross between parts.
Inputs may be any that keep to these rules, and one draw needn't show every extreme that they name: `neighbours`: cluster c lies in layer c // 5 of 16 periodic layers; its 14 blocks name distinct clusters of its own layer and the two layers beside it, wrapping at the ends. `cluster_atoms`: the clusters of layer j hold the atoms 5 * 64 * j to 5 * 64 * (j + 1) - 1, each once. `config_order`: each ensemble index once.
All inputs are finite; a program needn't handle non-finite values.
Results may differ from a plain program's by a relative error of at most 0.0085.
Values may be sent and summed in bfloat16 or wider, within the bound.
No kernel may reach another device: no remote copies, remote signals or barrier semaphores. Data moves between devices by JAX's collectives and lax.ppermute only.
A program may use at most 128 MiB of HBM per device.

v0:
```python
import jax
import jax.numpy as jnp
from jax import lax
from jax.sharding import PartitionSpec as P

ATOMS = 64
LAYER = 5


def with_halo(block, sides, width):
    for axis, dim in sides:
        count = lax.axis_size(axis)
        forward = [(i, i + 1) for i in range(count - 1)]
        forward.append((count - 1, 0))
        backward = [(target, source) for source, target in forward]
        low = lax.ppermute(
            lax.slice_in_dim(block, block.shape[dim] - width, None, axis=dim), axis, forward
        )
        high = lax.ppermute(lax.slice_in_dim(block, 0, width, axis=dim), axis, backward)
        block = jnp.concatenate([low, block, high], axis=dim)
    return block


def arrange(field, atom_map):
    picked = jnp.take(field, atom_map.reshape(-1), axis=2)
    picked = picked.reshape(field.shape[0], 3, atom_map.shape[0], atom_map.shape[1])
    return jnp.transpose(picked, (2, 1, 3, 0)).reshape(
        atom_map.shape[0], 3 * atom_map.shape[1], field.shape[0]
    )


def shards(displacements, forces, phi, neighbours, cluster_atoms, config_order, weights):
    axis_width = lax.axis_size("cx")
    position = lax.axis_index("cx")
    atom_local = cluster_atoms - position * (LAYER * ATOMS)
    layer_of = neighbours // LAYER
    offset = (layer_of - position + 1 + axis_width) % axis_width
    near_index = offset * LAYER + neighbours % LAYER
    moved_disp, moved_force = (
        lax.all_to_all(displacements, "cx", split_axis=2, concat_axis=0, tiled=True),
        lax.all_to_all(forces, "cx", split_axis=2, concat_axis=0, tiled=True),
    )
    cluster_force = arrange(moved_force, atom_local)
    cluster_disp = arrange(moved_disp, atom_local)
    framed_disp = with_halo(cluster_disp, (("cx", 0),), LAYER)
    beside_disp = jnp.take(framed_disp, near_index, axis=0)
    harmonic = jnp.einsum("ckij,ckjs->cis", phi, beside_disp, preferred_element_type=jnp.float32)
    residual = (cluster_force.astype(jnp.float32) + harmonic).astype(jnp.bfloat16)
    framed_resid = with_halo(residual, (("cx", 0),), LAYER)
    beside_resid = jnp.take(framed_resid, near_index, axis=0)
    match = config_order[:, None] == jnp.arange(config_order.shape[0], dtype=jnp.int32)[None, :]
    weight_row = jnp.sum(
        jnp.where(match, weights[None, :], jnp.zeros_like(weights)[None, :]), axis=1
    )
    wres = (residual.astype(jnp.float32) * weight_row[None, None, :]).astype(jnp.bfloat16)
    wdisp = (cluster_disp.astype(jnp.float32) * weight_row[None, None, :]).astype(jnp.bfloat16)
    first = jnp.einsum("cis,ckjs->ckij", wres, beside_disp, preferred_element_type=jnp.float32)
    second = jnp.einsum("cis,ckjs->ckij", wdisp, beside_resid, preferred_element_type=jnp.float32)
    summed = first + second
    gradient = (0.5 * summed).astype(jnp.bfloat16)
    return (residual, gradient)


def solution(mesh):
    in_specs = (
        P(("groups", "cx"), None, None),
        P(("groups", "cx"), None, None),
        P(("groups", "cx"), None, None, None),
        P("cx", None),
        P("cx", None),
        P("groups"),
        P("groups"),
    )
    out_specs = (P(("groups", "cx"), None, None), P(("groups", "cx"), None, None, None))
    return jax.shard_map(shards, mesh=mesh, in_specs=in_specs, out_specs=out_specs, check_vma=False)
```

profile of v0, /device:TPU:0, one launch (start us, length us, event | category | flops | bytes accessed | tf_op | source)
XLA Modules:
  0.0 138.1 jit_solution(12460175650179497296)
XLA Ops:
  0.6 0.0 copy-start.3
  0.6 0.0 copy-start.2
  0.6 6.5 %copy.46 = bf16[16,3,5120]{0,1,2:T(4,128)(2,1)} copy(bf16[16,3,5120]{2,0,1:T(8,128)(2,1)} %param.11) | data formatting | bytes 983040 | tf_op args[0]
  7.1 8.1 %reshape.93 = bf16[16,2,7680]{2,1,0:T(2,128)(2,1)} reshape(bf16[5120,3,16]{2,1,0:T(4,128)(2,1)} %bitcast.54) | data formatting | bytes 983040
  15.2 0.0 copy-start.4
  15.2 0.0 copy-start.5
  15.2 0.0 copy-start.6
  15.2 7.6 %all-to-all-start.1 = ((bf16[16,2,7680]{2,1,0:T(2,128)(2,1)}), bf16[16,2,7680]{2,1,0:T(2,128)(2,1)S(1)}, u32[]{:S(2)}, u32[]{:S(2)}) async-start(bf16[16,2,7680]{2,1,0:T(2,128)(2,1)} %reshape.93), calls=%async_computation.1 | async-start | bytes 983040 | tf_op jit(solution)/shard_map/all_to_all | solution.py:40
  22.8 0.0 copy-done.3
  22.8 0.1 reshape.33
  22.9 0.0 copy-done.2
  22.9 4.9 %copy.41 = bf16[16,3,5120]{0,1,2:T(4,128)(2,1)} copy(bf16[16,3,5120]{2,0,1:T(8,128)(2,1)S(1)} %copy-done.2) | data formatting | bytes 983040 | tf_op args[1]
  27.8 8.1 %reshape.91 = bf16[16,2,7680]{2,1,0:T(2,128)(2,1)} reshape(bf16[5120,3,16]{2,1,0:T(4,128)(2,1)} %bitcast.55) | data formatting | bytes 983040
  35.9 0.0 copy-done.4
  36.0 0.6 all-to-all-done.1
  36.5 5.5 %all-to-all-start = ((bf16[16,2,7680]{2,1,0:T(2,128)(2,1)}), bf16[16,2,7680]{2,1,0:T(2,128)(2,1)S(1)}, u32[]{:S(2)}, u32[]{:S(2)}) async-start(bf16[16,2,7680]{2,1,0:T(2,128)(2,1)} %reshape.91), calls=%async_computation | async-start | bytes 983040 | tf_op jit(solution)/shard_map/all_to_all | solution.py:41
  42.0 0.1 reshape.80
  42.1 0.0 copy-done.5
  42.1 0.0 copy-done.6
  42.1 0.2 select_reduce_fusion
  42.3 6.4 %reshape.94 = bf16[5120,3,16]{2,1,0:T(4,128)(2,1)} reshape(bf16[16,2,7680]{2,1,0:T(2,128)(2,1)S(1)} %all-to-all-done.1) | data formatting | bytes 983040
  48.7 5.9 %copy.47 = bf16[16,3,16,320]{3,0,2,1:T(8,128)(2,1)S(1)} copy(bf16[16,3,16,320]{0,1,3,2:T(4,128)(2,1)} %bitcast.52) | data formatting | bytes 983040 | tf_op jit(solution)/shard_map/all_to_all | solution.py:40
  54.6 0.7 copy.48
  55.3 2.3 %gather_fusion.1 = bf16[320,256,3]{1,2,0:T(4,128)(2,1)S(1)} fusion(bf16[256,3,320]{0,1,2:T(4,128)(2,1)S(1)} %copy.48, s32[1024]{0:T(1024)S(1)} %pad_clamp_fusion.1), kind=kCustom, calls=%fused_computation.2.clone | custom fusion | bytes 984320 | tf_op jit(solution)/shard_map/jit(_take)/gather | solution.py:25
  57.6 1.1 select_bitcast_fusion
  58.8 0.1 copy.49
  58.9 4.4 %collective-permute-start.1 = (bf16[5,192,256]{2,1,0:T(8,128)(2,1)S(1)}, bf16[5,192,256]{2,1,0:T(8,128)(2,1)}, u32[]{:S(2)}, u32[]{:S(2)}) collective-permute-start(bf16[5,192,256]{2,1,0:T(8,128)(2,1)S(1)} %bitcast.56), channel_id=1, source_target_pairs={{1,0},{2,1},{3,2},{4,3},{5,4},{6,5},{7,6},{8,7},{9,8},{10,9},{11,1... | collective-permute-start | bytes 1474568 | tf_op jit(solution)/shard_map/ppermute | solution.py:19
  63.3 0.0 collective-permute-start
  63.3 0.0 all-to-all-done
  63.3 6.4 %reshape.92 = bf16[5120,3,16]{2,1,0:T(4,128)(2,1)} reshape(bf16[16,2,7680]{2,1,0:T(2,128)(2,1)S(1)} %all-to-all-done) | data formatting | bytes 983040
  69.7 5.9 %copy.42 = bf16[16,3,16,320]{3,0,2,1:T(8,128)(2,1)S(1)} copy(bf16[16,3,16,320]{0,1,3,2:T(4,128)(2,1)} %bitcast.53) | data formatting | bytes 983040 | tf_op jit(solution)/shard_map/all_to_all | solution.py:41
  75.6 0.7 copy.43
  76.3 2.3 %gather_fusion = bf16[320,256,3]{1,2,0:T(4,128)(2,1)S(1)} fusion(bf16[256,3,320]{0,1,2:T(4,128)(2,1)S(1)} %copy.43, s32[1024]{0:T(1024)S(1)} %pad_clamp_fusion.1), kind=kCustom, calls=%fused_computation.clone | custom fusion | bytes 984320 | tf_op jit(solution)/shard_map/jit(_take)/gather | solution.py:25
  78.6 0.1 copy_select_fusion
  78.7 0.1 convert_bitcast_fusion
  78.8 0.1 copy.45
  78.9 0.0 collective-permute-done.1
  78.9 0.0 collective-permute-done
  78.9 1.3 pad_maximum_fusion
  80.3 6.7 %gather_fusion.2 = bf16[70,192,256]{2,1,0:T(8,128)(2,1)} fusion(bf16[15,192,256]{2,1,0:T(8,128)(2,1)S(1)} %pad_maximum_fusion, s32[1024]{0:T(1024)S(1)} %pad_clamp_fusion), kind=kCustom, calls=%fused_computation.1.clone | custom fusion | bytes 13762840 | tf_op jit(solution)/shard_map/jit(_take)/gather | solution.py:46
  87.0 0.0 copy-start
  87.0 7.2 %fusion.12 = bf16[5,192,256]{2,1,0:T(8,128)(2,1)S(1)} fusion(f32[5,192,256]{2,1,0:T(8,128)S(1)} %bitcast.64, bf16[5,14,192,192]{3,2,1,0:T(8,128)(2,1)} %param.13, bf16[5,14,192,256]{3,2,1,0:T(8,128)(2,1)} %bitcast.50, pred[5,14]{1,0:T(8,128)(4,1)S(1)} %get-tuple-element.14), kind=kOutput, calls=%fused_computation.18 | convolution fusion | flops 1325137920 | bytes 13516870 | tf_op jit(solution)/shard_map/ckij,ckjs->cis/dot_general | solution.py:47
  94.2 0.0 copy-start.1
  94.2 4.5 %collective-permute-start.3 = (bf16[5,192,256]{2,1,0:T(8,128)(2,1)S(1)}, bf16[5,192,256]{2,1,0:T(8,128)(2,1)S(1)}, u32[]{:S(2)}, u32[]{:S(2)}) collective-permute-start(bf16[5,192,256]{2,1,0:T(8,128)(2,1)S(1)} %fusion.12), channel_id=1, source_target_pairs={{1,0},{2,1},{3,2},{4,3},{5,4},{6,5},{7,6},{8,7},{9,8},{10,9},{11,1... | collective-permute-start | bytes 1474568 | tf_op jit(solution)/shard_map/ppermute | solution.py:19
  98.7 0.0 collective-permute-start.2
  98.7 0.0 copy-done
  98.7 7.0 %fusion.2 = f32[5,14,192,192]{3,2,1,0:T(8,128)} fusion(bf16[5,14,192,256]{3,2,1,0:T(8,128)(2,1)S(1)} %bitcast.51, pred[5,14]{1,0:T(8,128)(4,1)S(1)} %get-tuple-element.14, bf16[5,192,256]{2,1,0:T(8,128)(2,1)S(1)} %fusion.12, f32[256]{0:T(256)S(1)} %select_reduce_fusion), kind=kOutput, calls=%fused_computation.8 | convolution fusion | flops 1325383680 | bytes 17695814 | tf_op jit(solution)/shard_map/cis,ckjs->ckij/dot_general | solution.py:57
  105.7 0.0 collective-permute-done.3
  105.7 4.0 %collective-permute-done.2 = bf16[5,192,256]{2,1,0:T(8,128)(2,1)S(1)} collective-permute-done((bf16[5,192,256]{2,1,0:T(8,128)(2,1)S(1)}, bf16[5,192,256]{2,1,0:T(8,128)(2,1)S(1)}, u32[]{:S(2)}, u32[]{:S(2)}) %collective-permute-start.2) | collective-permute-done | bytes 491552 | tf_op jit(solution)/shard_map/ppermute | solution.py:16
  109.6 0.0 copy-done.1
  109.6 0.2 pad_maximum_fusion.1
  109.8 6.7 %gather_fusion.3 = bf16[70,192,256]{2,1,0:T(8,128)(2,1)} fusion(bf16[15,192,256]{2,1,0:T(8,128)(2,1)S(1)} %pad_maximum_fusion.1, s32[1024]{0:T(1024)S(1)} %pad_clamp_fusion), kind=kCustom, calls=%fused_computation.3.clone | custom fusion | bytes 13762840 | tf_op jit(solution)/shard_map/jit(_take)/gather | solution.py:50
  116.5 11.6 %fusion.4 = bf16[5,14,192,192]{2,3,1,0:T(8,128)(2,1)} fusion(f32[5,14,192,192]{3,2,1,0:T(8,128)} %fusion.2, bf16[5,14,192,256]{3,2,1,0:T(8,128)(2,1)} %bitcast.49, pred[5,14]{1,0:T(8,128)(4,1)S(1)} %get-tuple-element.14, bf16[5,192,256]{2,1,0:T(8,128)(2,1)S(1)} %bitcast.59, f32[256]{0:T(256)S(1)} %select_reduce_fusion), kind=kOutput, calls=%fused_computation.10 | convolution fusion | flops 1333125120 | bytes 22856774 | tf_op jit(solution)/shard_map/cis,ckjs->ckij/dot_general | solution.py:58
  128.1 10.0 %copy.51 = bf16[5,14,192,192]{3,2,1,0:T(8,128)(2,1)} copy(bf16[5,14,192,192]{2,3,1,0:T(8,128)(2,1)} %fusion.4) | data formatting | bytes 10321920
  (7 shorter events, 0.1 us)
Async XLA Ops:
  0.6 22.2 %copy-start.3 = (s32[5,64]{1,0:T(8,128)S(1)}, s32[5,64]{1,0:T(8,128)}, u32[]{:S(2)}) copy-start(s32[5,64]{1,0:T(8,128)} %param.15) | copy-start | bytes 3844
  0.6 22.3 %copy-start.2 = (bf16[16,3,5120]{2,0,1:T(8,128)(2,1)S(1)}, bf16[16,3,5120]{2,0,1:T(8,128)(2,1)}, u32[]{:S(2)}) copy-start(bf16[16,3,5120]{2,0,1:T(8,128)(2,1)} %param.12) | copy-start | bytes 1474564
  15.2 20.7 %copy-start.4 = (s32[5,14]{1,0:T(8,128)S(1)}, s32[5,14]{1,0:T(8,128)}, u32[]{:S(2)}) copy-start(s32[5,14]{1,0:T(8,128)} %param.14) | copy-start | bytes 844
  15.2 26.9 %copy-start.5 = (f32[256]{0:T(256)S(1)}, f32[256]{0:T(256)}, u32[]{:S(2)}) copy-start(f32[256]{0:T(256)} %param.17) | copy-start | bytes 3076
  15.2 26.9 %copy-start.6 = (s32[256]{0:T(256)S(1)}, s32[256]{0:T(256)}, u32[]{:S(2)}) copy-start(s32[256]{0:T(256)} %param.16) | copy-start | bytes 3076
  15.2 21.3 %all-to-all-start.1 = ((bf16[16,2,7680]{2,1,0:T(2,128)(2,1)}), bf16[16,2,7680]{2,1,0:T(2,128)(2,1)S(1)}, u32[]{:S(2)}, u32[]{:S(2)}) async-start(bf16[16,2,7680]{2,1,0:T(2,128)(2,1)} %reshape.93), calls=%async_computation.1 | async-start | bytes 983040 | tf_op jit(solution)/shard_map/all_to_all | solution.py:40
  36.5 26.8 %all-to-all-start = ((bf16[16,2,7680]{2,1,0:T(2,128)(2,1)}), bf16[16,2,7680]{2,1,0:T(2,128)(2,1)S(1)}, u32[]{:S(2)}, u32[]{:S(2)}) async-start(bf16[16,2,7680]{2,1,0:T(2,128)(2,1)} %reshape.91), calls=%async_computation | async-start | bytes 983040 | tf_op jit(solution)/shard_map/all_to_all | solution.py:41
  58.9 20.0 %collective-permute-start.1 = (bf16[5,192,256]{2,1,0:T(8,128)(2,1)S(1)}, bf16[5,192,256]{2,1,0:T(8,128)(2,1)}, u32[]{:S(2)}, u32[]{:S(2)}) collective-permute-start(bf16[5,192,256]{2,1,0:T(8,128)(2,1)S(1)} %bitcast.56), channel_id=1, source_target_pairs={{1,0},{2,1},{3,2},{4,3},{5,4},{6,5},{7,6},{8,7},{9,8},{10,9},{11,1... | collective-permute-start | bytes 1474568 | tf_op jit(solution)/shard_map/ppermute | solution.py:19
  63.3 15.6 %collective-permute-start = (bf16[5,192,256]{2,1,0:T(8,128)(2,1)S(1)}, bf16[5,192,256]{2,1,0:T(8,128)(2,1)}, u32[]{:S(2)}, u32[]{:S(2)}) collective-permute-start(bf16[5,192,256]{2,1,0:T(8,128)(2,1)S(1)} %bitcast.57), channel_id=1, source_target_pairs={{0,1},{1,2},{2,3},{3,4},{4,5},{5,6},{6,7},{7,8},{8,9},{9,10},{10,1... | collective-permute-start | bytes 1474568 | tf_op jit(solution)/shard_map/ppermute | solution.py:16
  87.0 11.7 %copy-start = (bf16[70,192,256]{2,1,0:T(8,128)(2,1)S(1)}, bf16[70,192,256]{2,1,0:T(8,128)(2,1)}, u32[]{:S(2)}) copy-start(bf16[70,192,256]{2,1,0:T(8,128)(2,1)} %gather_fusion.2) | copy-start | bytes 20643844
  94.2 15.5 %copy-start.1 = (bf16[5,192,256]{2,1,0:T(8,128)(2,1)}, bf16[5,192,256]{2,1,0:T(8,128)(2,1)S(1)}, u32[]{:S(2)}) copy-start(bf16[5,192,256]{2,1,0:T(8,128)(2,1)S(1)} %fusion.12) | copy-start | bytes 1474564
  94.2 11.5 %collective-permute-start.3 = (bf16[5,192,256]{2,1,0:T(8,128)(2,1)S(1)}, bf16[5,192,256]{2,1,0:T(8,128)(2,1)S(1)}, u32[]{:S(2)}, u32[]{:S(2)}) collective-permute-start(bf16[5,192,256]{2,1,0:T(8,128)(2,1)S(1)} %fusion.12), channel_id=1, source_target_pairs={{1,0},{2,1},{3,2},{4,3},{5,4},{6,5},{7,6},{8,7},{9,8},{10,9},{11,1... | collective-permute-start | bytes 1474568 | tf_op jit(solution)/shard_map/ppermute | solution.py:19
  98.7 11.0 %collective-permute-start.2 = (bf16[5,192,256]{2,1,0:T(8,128)(2,1)S(1)}, bf16[5,192,256]{2,1,0:T(8,128)(2,1)S(1)}, u32[]{:S(2)}, u32[]{:S(2)}) collective-permute-start(bf16[5,192,256]{2,1,0:T(8,128)(2,1)S(1)} %fusion.12), channel_id=1, source_target_pairs={{0,1},{1,2},{2,3},{3,4},{4,5},{5,6},{6,7},{7,8},{8,9},{9,10},{10,1... | collective-permute-start | bytes 1474568 | tf_op jit(solution)/shard_map/ppermute | solution.py:16
where the time goes:
time: 140 us; the launch traced here: 138 us
  local copies, waits for them, and re-layouts  82 us (59%)
  matrix products  25.8 us (18%)
  starting transfers between devices  21.9 us (16%)
  waiting for transfers between devices  4.55 us (3%)
  other arithmetic  3.08 us (2%)
    unnamed x21, local copies, waits for them, and re-layouts  50.4 us
    dot_general x1, matrix products, shards(): jnp.einsum('cis,ckjs->ckij', wdisp, beside_resid, preferred_element_type=...  11.6 us
    ppermute x2, starting transfers between devices, with_halo(): lax.ppermute(lax.slice_in_dim(block, 0, width, axis=dim), axis, backward)  8.88 us
    all_to_all x1, starting transfers between devices, shards(): lax.all_to_all(displacements, 'cx', split_axis=2, concat_axis=0, tiled=True)  7.55 us
    dot_general x1, matrix products, shards(): jnp.einsum('ckij,ckjs->cis', phi, beside_disp, preferred_element_type=jnp...  7.16 us
    dot_general x1, matrix products, shards(): jnp.einsum('cis,ckjs->ckij', wres, beside_disp, preferred_element_type=jn...  6.97 us
    gather x1, local copies, waits for them, and re-layouts, shards(): beside_resid = jnp.take(framed_resid, near_index, axis=0)  6.72 us
    gather x1, local copies, waits for them, and re-layouts, shards(): beside_disp = jnp.take(framed_disp, near_index, axis=0)  6.72 us
  transfers between devices with their start and end apart: 6, of which 2 were waited for; matrix products, arithmetic and copies ran while one was open for 38% of the time, Pallas kernels for 0%

commit v1 on v0

--- a/solution.py
+++ b/solution.py
@@ -5,6 +5,16 @@
 
 ATOMS = 64
 LAYER = 5
+
+
+def _direct_matrix(local, on_dim, d_out):
+    mixed_arr = jnp.concatenate(
+        lax.all_to_all(
+            jnp.stack(jnp.split(local, lax.axis_size("cx"), axis=on_dim), axis=0), "cx", 0, 0
+        ),
+        axis=d_out,
+    )
+    return mixed_arr
 
 
 def with_halo(block, sides, width):
@@ -38,7 +48,7 @@
     near_index = offset * LAYER + neighbours % LAYER
     moved_disp, moved_force = (
         lax.all_to_all(displacements, "cx", split_axis=2, concat_axis=0, tiled=True),
-        lax.all_to_all(forces, "cx", split_axis=2, concat_axis=0, tiled=True),
+        _direct_matrix(forces, on_dim=2, d_out=0),
     )
     cluster_force = arrange(moved_force, atom_local)
     cluster_disp = arrange(moved_disp, atom_local)

time: 140 us -> 129 us (0.921)
  local copies, waits for them, and re-layouts: 82 us -> 67.2 us
  waiting for transfers between devices: 4.55 us -> 14.6 us
  starting transfers between devices: 21.9 us -> 16.4 us
    unnamed x21 -> x33, local copies, waits for them, and re-layouts: 50.4 us -> 40.8 us
    all_to_all x2 -> x1, local copies, waits for them, and re-layouts: 6.59 us -> 0.06 us  [_direct_matrix(): lax.all_to_all(jnp.stack(jnp.split(local, lax.axis_size('cx'), axis=on_di...]
    ppermute x2, waiting for transfers between devices: 3.98 us -> 8.52 us  [with_halo(): lax.ppermute(lax.slice_in_dim(block, block.shape[dim] - width, None, axis...]
    ppermute x2, starting transfers between devices: 8.88 us -> 4.54 us  [with_halo(): lax.ppermute(lax.slice_in_dim(block, 0, width, axis=dim), axis, backward)]
    ppermute x2, waiting for transfers between devices: 0.01 us -> 2.93 us  [with_halo(): lax.ppermute(lax.slice_in_dim(block, 0, width, axis=dim), axis, backward)]
    all_to_all x1, waiting for transfers between devices: 0.57 us -> 3.12 us  [shards(): lax.all_to_all(displacements, 'cx', split_axis=2, concat_axis=0, tiled=True)]
    all_to_all x1, starting transfers between devices: 5.45 us -> 3.99 us  [_direct_matrix(): lax.all_to_all(jnp.stack(jnp.split(local, lax.axis_size('cx'), axis=on_di...]
  transfers between devices with their start and end apart: 6 -> 6, of which waited for: 2 -> 4; matrix products, arithmetic and copies ran while one was open for 38% -> 30% of each run, Pallas kernels for 0% -> 0%
where the time goes in v1:
time: 129 us; the launch traced here: 128 us
  local copies, waits for them, and re-layouts  67.2 us (52%)
  matrix products  25.8 us (20%)
  starting transfers between devices  16.4 us (13%)
  waiting for transfers between devices  14.6 us (11%)
  other arithmetic  3.08 us (2%)
    unnamed x33, local copies, waits for them, and re-layouts  40.8 us
    dot_general x1, matrix products, shards(): jnp.einsum('cis,ckjs->ckij', wdisp, beside_resid, preferred_element_type=...  11.6 us
    ppermute x2, waiting for transfers between devices, with_halo(): lax.ppermute(lax.slice_in_dim(block, block.shape[dim] - width, None, axis...  8.52 us
    all_to_all x1, starting transfers between devices, shards(): lax.all_to_all(displacements, 'cx', split_axis=2, concat_axis=0, tiled=True)  7.41 us
    dot_general x1, matrix products, shards(): jnp.einsum('ckij,ckjs->cis', phi, beside_disp, preferred_element_type=jnp...  7.16 us
    dot_general x1, matrix products, shards(): jnp.einsum('cis,ckjs->ckij', wres, beside_disp, preferred_element_type=jn...  6.97 us
    gather x1, local copies, waits for them, and re-layouts, shards(): beside_resid = jnp.take(framed_resid, near_index, axis=0)  6.72 us
    gather x1, local copies, waits for them, and re-layouts, shards(): beside_disp = jnp.take(framed_disp, near_index, axis=0)  6.72 us
  transfers between devices with their start and end apart: 6, of which 4 were waited for; matrix products, arithmetic and copies ran while one was open for 30% of the time, Pallas kernels for 0%

profile of v1, /device:TPU:0, one launch (start us, length us, event | category | flops | bytes accessed | tf_op | source)
XLA Modules:
  0.0 127.9 jit_solution(17757981557728947074)
XLA Ops:
  0.6 0.0 copy-start.3
  0.6 0.0 copy-start.2
  0.7 0.0 copy-start.4
  0.7 0.0 copy-start.5
  0.7 0.0 copy-start.6
  0.7 6.5 %copy.43 = bf16[16,3,5120]{0,1,2:T(4,128)(2,1)} copy(bf16[16,3,5120]{2,0,1:T(8,128)(2,1)} %param.11) | data formatting | bytes 983040 | tf_op args[0]
  7.2 8.1 %reshape.95 = bf16[16,2,7680]{2,1,0:T(2,128)(2,1)} reshape(bf16[5120,3,16]{2,1,0:T(4,128)(2,1)} %bitcast.80) | data formatting | bytes 983040
  15.3 7.4 %all-to-all-start.1 = ((bf16[16,2,7680]{2,1,0:T(2,128)(2,1)}), bf16[16,2,7680]{2,1,0:T(2,128)(2,1)S(1)}, u32[]{:S(2)}, u32[]{:S(2)}) async-start(bf16[16,2,7680]{2,1,0:T(2,128)(2,1)} %reshape.95), calls=%async_computation.1 | async-start | bytes 983040 | tf_op jit(solution)/shard_map/all_to_all | solution.py:50
  22.7 0.0 copy-done.3
  22.7 0.0 copy-done.2
  22.7 0.6 bitcast_dynamic-update-slice_fusion.15
  23.4 0.7 bitcast_dynamic-update-slice_fusion.14
  24.1 0.6 bitcast_dynamic-update-slice_fusion.13
  24.7 0.7 bitcast_dynamic-update-slice_fusion.12
  25.4 0.6 bitcast_dynamic-update-slice_fusion.11
  26.0 0.7 bitcast_dynamic-update-slice_fusion.10
  26.7 0.6 bitcast_dynamic-update-slice_fusion.9
  27.3 0.7 bitcast_dynamic-update-slice_fusion.8
  28.0 0.6 bitcast_dynamic-update-slice_fusion.7
  28.6 0.7 bitcast_dynamic-update-slice_fusion.6
  29.3 0.6 bitcast_dynamic-update-slice_fusion.5
  29.9 0.7 bitcast_dynamic-update-slice_fusion.4
  30.6 0.0 copy-done.4
  30.6 0.1 reshape.37
  30.7 0.6 bitcast_dynamic-update-slice_fusion.3
  31.3 0.7 bitcast_dynamic-update-slice_fusion.2
  32.0 0.6 bitcast_dynamic-update-slice_fusion.1
  32.6 0.7 bitcast_dynamic-update-slice_fusion
  33.3 3.1 %all-to-all-done.1 = bf16[16,2,7680]{2,1,0:T(2,128)(2,1)S(1)} async-done(((bf16[16,2,7680]{2,1,0:T(2,128)(2,1)}), bf16[16,2,7680]{2,1,0:T(2,128)(2,1)S(1)}, u32[]{:S(2)}, u32[]{:S(2)}) %all-to-all-start.1) | async-done | bytes 491552 | tf_op jit(solution)/shard_map/all_to_all | solution.py:50
  36.4 4.0 %all-to-all-start = ((bf16[16,16,3,320]{3,1,2,0:T(8,128)(2,1)}), bf16[16,16,3,320]{3,1,2,0:T(8,128)(2,1)S(1)}, u32[]{:S(2)}, u32[]{:S(2)}) async-start(bf16[16,16,3,320]{3,1,2,0:T(8,128)(2,1)} %bitcast_dynamic-update-slice_fusion), calls=%async_computation | async-start | bytes 1179648 | tf_op jit(solution)/shard_map/all_to_all | solution.py:12
  40.4 0.1 reshape.84
  40.5 0.0 copy-done.5
  40.5 0.0 copy-done.6
  40.5 0.2 select_reduce_fusion
  40.7 6.4 %reshape.96 = bf16[5120,3,16]{2,1,0:T(4,128)(2,1)} reshape(bf16[16,2,7680]{2,1,0:T(2,128)(2,1)S(1)} %all-to-all-done.1) | data formatting | bytes 983040
  47.1 5.9 %copy.44 = bf16[16,3,16,320]{3,0,2,1:T(8,128)(2,1)S(1)} copy(bf16[16,3,16,320]{0,1,3,2:T(4,128)(2,1)} %bitcast.79) | data formatting | bytes 983040 | tf_op jit(solution)/shard_map/all_to_all | solution.py:50
  53.0 0.7 copy.45
  53.7 2.3 %gather_fusion.1 = bf16[320,256,3]{1,2,0:T(4,128)(2,1)S(1)} fusion(bf16[256,3,320]{0,1,2:T(4,128)(2,1)S(1)} %copy.45, s32[1024]{0:T(1024)S(1)} %pad_clamp_fusion.1), kind=kCustom, calls=%fused_computation.2.clone | custom fusion | bytes 984320 | tf_op jit(solution)/shard_map/jit(_take)/gather | solution.py:35
  56.1 1.1 select_bitcast_fusion
  57.2 0.1 copy.46
  57.3 4.4 %collective-permute-start.1 = (bf16[5,192,256]{2,1,0:T(8,128)(2,1)S(1)}, bf16[5,192,256]{2,1,0:T(8,128)(2,1)}, u32[]{:S(2)}, u32[]{:S(2)}) collective-permute-start(bf16[5,192,256]{2,1,0:T(8,128)(2,1)S(1)} %bitcast.81), channel_id=1, source_target_pairs={{1,0},{2,1},{3,2},{4,3},{5,4},{6,5},{7,6},{8,7},{9,8},{10,9},{11,1... | collective-permute-start | bytes 1474568 | tf_op jit(solution)/shard_map/ppermute | solution.py:29
  61.7 0.0 collective-permute-start
  61.7 0.0 all-to-all-done
  61.7 0.1 copy.39
  61.8 0.7 copy.40
  62.5 2.3 %gather_fusion = bf16[320,256,3]{1,2,0:T(4,128)(2,1)S(1)} fusion(bf16[256,3,320]{0,1,2:T(4,128)(2,1)S(1)} %copy.40, s32[1024]{0:T(1024)S(1)} %pad_clamp_fusion.1), kind=kCustom, calls=%fused_computation.clone | custom fusion | bytes 984320 | tf_op jit(solution)/shard_map/jit(_take)/gather | solution.py:35
  64.8 0.1 copy_select_fusion
  64.9 0.1 convert_bitcast_fusion
  65.0 0.1 copy.42
  65.1 2.9 %collective-permute-done.1 = bf16[5,192,256]{2,1,0:T(8,128)(2,1)} collective-permute-done((bf16[5,192,256]{2,1,0:T(8,128)(2,1)S(1)}, bf16[5,192,256]{2,1,0:T(8,128)(2,1)}, u32[]{:S(2)}, u32[]{:S(2)}) %collective-permute-start.1) | collective-permute-done | bytes 491552 | tf_op jit(solution)/shard_map/ppermute | solution.py:29
  68.1 4.7 %collective-permute-done = bf16[5,192,256]{2,1,0:T(8,128)(2,1)} collective-permute-done((bf16[5,192,256]{2,1,0:T(8,128)(2,1)S(1)}, bf16[5,192,256]{2,1,0:T(8,128)(2,1)}, u32[]{:S(2)}, u32[]{:S(2)}) %collective-permute-start) | collective-permute-done | bytes 491552 | tf_op jit(solution)/shard_map/ppermute | solution.py:26
  72.8 1.3 %pad_maximum_fusion = bf16[15,192,256]{2,1,0:T(8,128)(2,1)S(1)} fusion(bf16[5,192,256]{2,1,0:T(8,128)(2,1)} %collective-permute-done.1, bf16[5,192,256]{2,1,0:T(8,128)(2,1)S(1)} %bitcast.83, bf16[5,192,256]{2,1,0:T(8,128)(2,1)} %collective-permute-done), kind=kLoop, calls=%fused_computation.14 | loop fusion | flops 1474560 | bytes 2949120 | tf_op jit(solution)/shard_map/concatenate | solution.py:30
  74.1 6.7 %gather_fusion.2 = bf16[70,192,256]{2,1,0:T(8,128)(2,1)} fusion(bf16[15,192,256]{2,1,0:T(8,128)(2,1)S(1)} %pad_maximum_fusion, s32[1024]{0:T(1024)S(1)} %pad_clamp_fusion), kind=kCustom, calls=%fused_computation.1.clone | custom fusion | bytes 13762840 | tf_op jit(solution)/shard_map/jit(_take)/gather | solution.py:56
  80.8 7.2 %fusion.12 = bf16[5,192,256]{2,1,0:T(8,128)(2,1)S(1)} fusion(f32[5,192,256]{2,1,0:T(8,128)S(1)} %bitcast.89, bf16[5,14,192,192]{3,2,1,0:T(8,128)(2,1)} %param.13, bf16[5,14,192,256]{3,2,1,0:T(8,128)(2,1)} %bitcast.77, pred[5,14]{1,0:T(8,128)(4,1)S(1)} %get-tuple-element.14), kind=kOutput, calls=%fused_computation.18 | convolution fusion | flops 1325137920 | bytes 13516870 | tf_op jit(solution)/shard_map/ckij,ckjs->cis/dot_general | solution.py:57
  88.0 0.0 copy-start.1
  88.0 0.1 collective-permute-start.3
  88.2 0.4 collective-permute-start.2
  88.6 7.0 %fusion.2 = f32[5,14,192,192]{3,2,1,0:T(8,128)} fusion(bf16[5,14,192,256]{3,2,1,0:T(8,128)(2,1)S(1)} %bitcast.78, pred[5,14]{1,0:T(8,128)(4,1)S(1)} %get-tuple-element.14, bf16[5,192,256]{2,1,0:T(8,128)(2,1)S(1)} %fusion.12, f32[256]{0:T(256)S(1)} %select_reduce_fusion), kind=kOutput, calls=%fused_computation.8 | convolution fusion | flops 1325383680 | bytes 17695814 | tf_op jit(solution)/shard_map/cis,ckjs->ckij/dot_general | solution.py:67
  95.6 0.0 collective-permute-done.3
  95.6 3.8 %collective-permute-done.2 = bf16[5,192,256]{2,1,0:T(8,128)(2,1)S(1)} collective-permute-done((bf16[5,192,256]{2,1,0:T(8,128)(2,1)S(1)}, bf16[5,192,256]{2,1,0:T(8,128)(2,1)S(1)}, u32[]{:S(2)}, u32[]{:S(2)}) %collective-permute-start.2) | collective-permute-done | bytes 491552 | tf_op jit(solution)/shard_map/ppermute | solution.py:26
  99.4 0.2 pad_maximum_fusion.1
  99.5 6.7 %gather_fusion.3 = bf16[70,192,256]{2,1,0:T(8,128)(2,1)} fusion(bf16[15,192,256]{2,1,0:T(8,128)(2,1)S(1)} %pad_maximum_fusion.1, s32[1024]{0:T(1024)S(1)} %pad_clamp_fusion), kind=kCustom, calls=%fused_computation.3.clone | custom fusion | bytes 13762840 | tf_op jit(solution)/shard_map/jit(_take)/gather | solution.py:60
  106.3 11.6 %fusion.4 = bf16[5,14,192,192]{2,3,1,0:T(8,128)(2,1)} fusion(f32[5,14,192,192]{3,2,1,0:T(8,128)} %fusion.2, bf16[5,14,192,256]{3,2,1,0:T(8,128)(2,1)} %bitcast.76, pred[5,14]{1,0:T(8,128)(4,1)S(1)} %get-tuple-element.14, bf16[5,192,256]{2,1,0:T(8,128)(2,1)S(1)} %bitcast.84, f32[256]{0:T(256)S(1)} %select_reduce_fusion), kind=kOutput, calls=%fused_computation.10 | convolution fusion | flops 1333125120 | bytes 22856774 | tf_op jit(solution)/shard_map/cis,ckjs->ckij/dot_general | solution.py:68
  117.9 10.0 %copy.48 = bf16[5,14,192,192]{3,2,1,0:T(8,128)(2,1)} copy(bf16[5,14,192,192]{2,3,1,0:T(8,128)(2,1)} %fusion.4) | data formatting | bytes 10321920
  (10 shorter events, 0.1 us)
Async XLA Ops:
  0.6 22.1 %copy-start.3 = (s32[5,14]{1,0:T(8,128)S(1)}, s32[5,14]{1,0:T(8,128)}, u32[]{:S(2)}) copy-start(s32[5,14]{1,0:T(8,128)} %param.14) | copy-start | bytes 844
  0.6 22.1 %copy-start.2 = (bf16[16,3,5120]{2,0,1:T(8,128)(2,1)S(1)}, bf16[16,3,5120]{2,0,1:T(8,128)(2,1)}, u32[]{:S(2)}) copy-start(bf16[16,3,5120]{2,0,1:T(8,128)(2,1)} %param.12) | copy-start | bytes 1474564
  0.7 30.0 %copy-start.4 = (s32[5,64]{1,0:T(8,128)S(1)}, s32[5,64]{1,0:T(8,128)}, u32[]{:S(2)}) copy-start(s32[5,64]{1,0:T(8,128)} %param.15) | copy-start | bytes 3844
  0.7 39.9 %copy-start.5 = (f32[256]{0:T(256)S(1)}, f32[256]{0:T(256)}, u32[]{:S(2)}) copy-start(f32[256]{0:T(256)} %param.17) | copy-start | bytes 3076
  0.7 39.9 %copy-start.6 = (s32[256]{0:T(256)S(1)}, s32[256]{0:T(256)}, u32[]{:S(2)}) copy-start(s32[256]{0:T(256)} %param.16) | copy-start | bytes 3076
  15.3 21.2 %all-to-all-start.1 = ((bf16[16,2,7680]{2,1,0:T(2,128)(2,1)}), bf16[16,2,7680]{2,1,0:T(2,128)(2,1)S(1)}, u32[]{:S(2)}, u32[]{:S(2)}) async-start(bf16[16,2,7680]{2,1,0:T(2,128)(2,1)} %reshape.95), calls=%async_computation.1 | async-start | bytes 983040 | tf_op jit(solution)/shard_map/all_to_all | solution.py:50
  36.4 25.3 %all-to-all-start = ((bf16[16,16,3,320]{3,1,2,0:T(8,128)(2,1)}), bf16[16,16,3,320]{3,1,2,0:T(8,128)(2,1)S(1)}, u32[]{:S(2)}, u32[]{:S(2)}) async-start(bf16[16,16,3,320]{3,1,2,0:T(8,128)(2,1)} %bitcast_dynamic-update-slice_fusion), calls=%async_computation | async-start | bytes 1179648 | tf_op jit(solution)/shard_map/all_to_all | solution.py:12
  57.3 10.7 %collective-permute-start.1 = (bf16[5,192,256]{2,1,0:T(8,128)(2,1)S(1)}, bf16[5,192,256]{2,1,0:T(8,128)(2,1)}, u32[]{:S(2)}, u32[]{:S(2)}) collective-permute-start(bf16[5,192,256]{2,1,0:T(8,128)(2,1)S(1)} %bitcast.81), channel_id=1, source_target_pairs={{1,0},{2,1},{3,2},{4,3},{5,4},{6,5},{7,6},{8,7},{9,8},{10,9},{11,1... | collective-permute-start | bytes 1474568 | tf_op jit(solution)/shard_map/ppermute | solution.py:29
  61.7 11.1 %collective-permute-start = (bf16[5,192,256]{2,1,0:T(8,128)(2,1)S(1)}, bf16[5,192,256]{2,1,0:T(8,128)(2,1)}, u32[]{:S(2)}, u32[]{:S(2)}) collective-permute-start(bf16[5,192,256]{2,1,0:T(8,128)(2,1)S(1)} %bitcast.82), channel_id=1, source_target_pairs={{0,1},{1,2},{2,3},{3,4},{4,5},{5,6},{6,7},{7,8},{8,9},{9,10},{10,1... | collective-permute-start | bytes 1474568 | tf_op jit(solution)/shard_map/ppermute | solution.py:26
  80.8 7.7 %copy-start = (bf16[70,192,256]{2,1,0:T(8,128)(2,1)S(1)}, bf16[70,192,256]{2,1,0:T(8,128)(2,1)}, u32[]{:S(2)}) copy-start(bf16[70,192,256]{2,1,0:T(8,128)(2,1)} %gather_fusion.2) | copy-start | bytes 20643844
  88.0 11.4 %copy-start.1 = (bf16[5,192,256]{2,1,0:T(8,128)(2,1)}, bf16[5,192,256]{2,1,0:T(8,128)(2,1)S(1)}, u32[]{:S(2)}) copy-start(bf16[5,192,256]{2,1,0:T(8,128)(2,1)S(1)} %fusion.12) | copy-start | bytes 1474564
  88.0 7.5 %collective-permute-start.3 = (bf16[5,192,256]{2,1,0:T(8,128)(2,1)S(1)}, bf16[5,192,256]{2,1,0:T(8,128)(2,1)S(1)}, u32[]{:S(2)}, u32[]{:S(2)}) collective-permute-start(bf16[5,192,256]{2,1,0:T(8,128)(2,1)S(1)} %fusion.12), channel_id=1, source_target_pairs={{1,0},{2,1},{3,2},{4,3},{5,4},{6,5},{7,6},{8,7},{9,8},{10,9},{11,1... | collective-permute-start | bytes 1474568 | tf_op jit(solution)/shard_map/ppermute | solution.py:29
  88.2 11.2 %collective-permute-start.2 = (bf16[5,192,256]{2,1,0:T(8,128)(2,1)S(1)}, bf16[5,192,256]{2,1,0:T(8,128)(2,1)S(1)}, u32[]{:S(2)}, u32[]{:S(2)}) collective-permute-start(bf16[5,192,256]{2,1,0:T(8,128)(2,1)S(1)} %fusion.12), channel_id=1, source_target_pairs={{0,1},{1,2},{2,3},{3,4},{4,5},{5,6},{6,7},{7,8},{8,9},{9,10},{10,1... | collective-permute-start | bytes 1474568 | tf_op jit(solution)/shard_map/ppermute | solution.py:26
